TPU v7x, 32 devices: a whole 2x2x4 slice. The times are simulated.
32 devices in a mesh: dp: 16 (over z, x, core), tp: 2 (over y).
Axes of the slice: x: 2, y: 2, z: 4, core: 2. Of those that a mesh axis runs over, the one named last changes fastest.
Arguments:
- inputs: bfloat16 [32768, 640], P('dp'), may hold values from -6 to 6
- out_grad: bfloat16 [32768, 640], P('dp'), may hold values from -6 to 6
- segment_ids: int32 [32, 1024], P('dp'), may hold values from 0 to 5, never falling along the last dimension, each value on 1 to 400 neighbouring positions
- attn_weights: float32 [4, 640, 640], P(None, 'dp', 'tp'), may hold values from -6 to 6
- ffn_weights: float32 [2, 640, 2560], P(None, 'dp', 'tp'), may hold values from -4 to 4
- head_bias: float32 [3, 640], P(None, 'tp'), may hold values from -1 to 1
- hidden_bias: float32 [2560], P('tp'), may hold values from -1 to 1
- norm_vectors: float32 [6, 640], replicated, may hold values from -1 to 2
- attn_first: float32 [4, 640, 640], P(None, 'dp', 'tp')
- ffn_first: float32 [2, 640, 2560], P(None, 'dp', 'tp')
- head_first: float32 [3, 640], P(None, 'tp')
- hidden_first: float32 [2560], P('tp')
- vector_first: float32 [6, 640], replicated
- attn_second: float32 [4, 640, 640], P(None, 'dp', 'tp')
- ffn_second: float32 [2, 640, 2560], P(None, 'dp', 'tp')
- head_second: float32 [3, 640], P(None, 'tp')
- hidden_second: float32 [2560], P('tp')
- vector_second: float32 [6, 640], replicated
Outputs:
- layer_output: bfloat16 [32768, 640], P('dp')
- input_grad: bfloat16 [32768, 640], P('dp')
- new_attn_weights: float32 [4, 640, 640], P(None, 'dp', 'tp')
- new_ffn_weights: float32 [2, 640, 2560], P(None, 'dp', 'tp')
- new_head_bias: float32 [3, 640], P(None, 'tp')
- new_hidden_bias: float32 [2560], P('tp')
- new_norm_vectors: float32 [6, 640], replicated
- attn_first_new: float32 [4, 640, 640], P(None, 'dp', 'tp')
- ffn_first_new: float32 [2, 640, 2560], P(None, 'dp', 'tp')
- head_first_new: float32 [3, 640], P(None, 'tp')
- hidden_first_new: float32 [2560], P('tp')
- vector_first_new: float32 [6, 640], replicated
- attn_second_new: float32 [3, 640, 640], P(None, 'dp', 'tp')
- out_second_new: float32 [640, 640], P('dp', 'tp')
- ffn_second_new: float32 [2, 640, 2560], P(None, 'dp', 'tp')
- head_second_new: float32 [3, 640], P(None, 'tp')
- hidden_second_new: float32 [2560], P('tp')
- vector_second_new: float32 [4, 640], replicated
- norm_second_new: float32 [2, 640], replicated
- trust_norms: float32 [2, 16], replicated
Inputs may be any that keep to these rules, and one draw needn't show every extreme that they name: `segment_ids`: within each row of 1024 slots the ids never fall; each of the 6 ids forms one run of 1 to 400 slots, and one run has exactly 400 slots.
All inputs are finite; a program needn't handle non-finite values.
Results may differ from a plain program's by a relative error of at most 0.019.
Values may be sent and summed in bfloat16 or wider, within the bound.
No kernel may reach another device: no remote copies, remote signals or barrier semaphores. Data moves between devices by JAX's collectives and lax.ppermute only.
A program may use at most 192 MiB of HBM per device.

v0:
```python
from functools import partial
import jax
import jax.numpy as jnp
from jax import lax
from jax.sharding import PartitionSpec as P

HD = 32
STEP = 10
EPS_NORM = 1e-05
EPS_ADAM = 1e-06
BETA_ONE = 0.9
BETA_TWO = 0.999
DECAY = 0.01
RATE = 0.5
MASKED = -1e30


def layer_norm(values, scale_gain, offset):
    average = jnp.mean(values, axis=-1, keepdims=True)
    centered = values - average
    variance = jnp.mean(centered * centered, axis=-1, keepdims=True)
    return centered * lax.rsqrt(variance + EPS_NORM) * scale_gain + offset


def rope_tables(segments):
    slots_index = jnp.arange(segments.shape[0], dtype=jnp.int32)
    before = jnp.sum((segments[None, :] < segments[:, None]).astype(jnp.int32), axis=1)
    position = (slots_index - before).astype(jnp.float32)
    frequency = 10000.0 ** (-jnp.arange(0, HD, 2).astype(jnp.float32) / HD)
    angles = position[:, None] * frequency[None, :]
    angles = jnp.concatenate([angles, angles], axis=-1)
    return (jnp.cos(angles), jnp.sin(angles))


def rotate(values, cosine_table, sine_table):
    middle = values.shape[-1] // 2
    turned = jnp.concatenate([-values[..., middle:], values[..., :middle]], axis=-1)
    return values * cosine_table + turned * sine_table


def block_scores(queries, keys_row, same_protein):
    scores = jnp.einsum(
        "qhd,khd->hqk", queries, keys_row, preferred_element_type=jnp.float32
    ) * HD ** (-0.5)
    return jnp.where(same_protein[None], scores, MASKED)


def attend_block(queries, keys_row, values_row, same_protein):
    scores = block_scores(queries, keys_row, same_protein)
    highest = jnp.max(scores, axis=-1, keepdims=True)
    weights_exp = jnp.exp(scores - highest)
    row_total = jnp.sum(weights_exp, axis=-1, keepdims=True)
    attention = (weights_exp / row_total).astype(jnp.bfloat16)
    heads_out = jnp.einsum(
        "hqk,khd->qhd", attention, values_row, preferred_element_type=jnp.float32
    )
    return (heads_out, (highest + jnp.log(row_total))[..., 0])


def attend_block_back(queries, keys_row, values_row, same_protein, log_total, grad_heads):
    scores = block_scores(queries, keys_row, same_protein)
    attention = jnp.exp(scores - log_total[..., None])
    grad_values = jnp.einsum(
        "hqk,qhd->khd",
        attention.astype(jnp.bfloat16),
        grad_heads,
        preferred_element_type=jnp.float32,
    )
    grad_attention = jnp.einsum(
        "qhd,khd->hqk", grad_heads, values_row, preferred_element_type=jnp.float32
    )
    center = jnp.sum(attention * grad_attention, axis=-1, keepdims=True)
    grad_scores = (attention * (grad_attention - center)).astype(jnp.bfloat16)
    grad_queries = jnp.einsum(
        "hqk,khd->qhd", grad_scores, keys_row, preferred_element_type=jnp.float32
    ) * HD ** (-0.5)
    grad_keys = jnp.einsum(
        "hqk,qhd->khd", grad_scores, queries, preferred_element_type=jnp.float32
    ) * HD ** (-0.5)
    return (grad_queries, grad_keys, grad_values)


def attend_row(queries, keys_row, values_row, segments, block_rows):
    blocks = segments.shape[0] // block_rows
    query_blocks = queries.reshape((blocks, block_rows) + queries.shape[1:])
    segment_blocks = segments.reshape(blocks, block_rows)

    def one_block(packed):
        same_protein = packed[1][:, None] == segments[None, :]
        return attend_block(packed[0], keys_row, values_row, same_protein)

    heads_out, log_total = lax.map(one_block, (query_blocks, segment_blocks))
    return (heads_out.reshape(queries.shape), log_total)


def attend_row_back(queries, keys_row, values_row, segments, log_total, grad_heads, block_rows):
    blocks = segments.shape[0] // block_rows
    query_blocks = queries.reshape((blocks, block_rows) + queries.shape[1:])
    grad_blocks = grad_heads.reshape((blocks, block_rows) + grad_heads.shape[1:])
    segment_blocks = segments.reshape(blocks, block_rows)

    def one_block(totals, packed):
        same_protein = packed[1][:, None] == segments[None, :]
        grad_queries, grad_keys, grad_values = attend_block_back(
            packed[0], keys_row, values_row, same_protein, packed[2], packed[3]
        )
        return ((totals[0] + grad_keys, totals[1] + grad_values), grad_queries)

    zeros_rows = jnp.zeros(keys_row.shape, jnp.float32)
    sums_kv, grad_queries = lax.scan(
        one_block, (zeros_rows, zeros_rows), (query_blocks, segment_blocks, log_total, grad_blocks)
    )
    return (grad_queries.reshape(queries.shape), sums_kv[0], sums_kv[1])


def lamb_moments(weight, gradient, moment_one, moment_two):
    first_new = BETA_ONE * moment_one + (1.0 - BETA_ONE) * gradient
    second_new = BETA_TWO * moment_two + (1.0 - BETA_TWO) * gradient * gradient
    corrected = first_new / (1.0 - BETA_ONE**STEP)
    variance = second_new / (1.0 - BETA_TWO**STEP)
    update = corrected / (jnp.sqrt(variance) + EPS_ADAM) + DECAY * weight
    return (first_new, second_new, update)


def sum_squares(array):
    return jnp.sum(array * array, axis=tuple(range(1, array.ndim)))


def on_device(
    inputs,
    out_grad,
    segment_ids,
    attn_weights,
    ffn_weights,
    head_bias,
    hidden_bias,
    norm_vectors,
    attn_first,
    ffn_first,
    head_first,
    hidden_first,
    vector_first,
    attn_second,
    ffn_second,
    head_second,
    hidden_second,
    vector_second,
):
    data_count = lax.axis_size("dp")
    tensor_count = lax.axis_size("tp")
    row_count, slot_count = segment_ids.shape
    token_count = row_count * slot_count
    head_width = attn_weights.shape[2]
    local_heads = head_width // HD
    block_rows = min(512, slot_count)
    shard_rows = attn_weights.shape[1]
    masters = [attn_weights, ffn_weights, head_bias, hidden_bias.reshape(1, -1), norm_vectors]
    replicas = [1.0, 1.0, 1.0 / data_count, 1.0 / data_count, 1.0 / (data_count * tensor_count)]
    weight_terms = jnp.concatenate(
        [sum_squares(masters[member]) * replicas[member] for member in range(5)]
    )
    weight_sums = lax.psum(weight_terms, ("dp", "tp"))
    gathered_attn, gathered_ffn = (
        lax.all_gather(attn_weights.astype(jnp.bfloat16), "dp", axis=1, tiled=True),
        lax.all_gather(ffn_weights.astype(jnp.bfloat16), "dp", axis=1, tiled=True),
    )
    tables = jax.vmap(rope_tables)(segment_ids)
    cosine_table = tables[0][:, :, None, :]
    sine_table = tables[1][:, :, None, :]
    features = inputs.astype(jnp.float32)
    normed, norm_back = jax.vjp(layer_norm, features, norm_vectors[0], norm_vectors[1])
    normed_low = normed.astype(jnp.bfloat16)
    projected = jnp.einsum(
        "td,cdw->ctw", normed_low, gathered_attn[:3], preferred_element_type=jnp.float32
    )
    projected = projected + head_bias[:, None, :]
    shaped = projected.reshape(3, row_count, slot_count, local_heads, HD)
    turned, rotate_back = jax.vjp(lambda pair: rotate(pair, cosine_table, sine_table), shaped[:2])
    turned_low = turned.astype(jnp.bfloat16)
    values_low = shaped[2].astype(jnp.bfloat16)
    heads_out, log_total = lax.map(
        lambda packed: attend_row(packed[0], packed[1], packed[2], packed[3], block_rows),
        (turned_low[0], turned_low[1], values_low, segment_ids),
    )
    heads_low = heads_out.reshape(token_count, head_width).astype(jnp.bfloat16)
    out_projection = gathered_attn[3]
    attended = lax.psum(
        jnp.einsum(
            "tw,dw->td", heads_low, out_projection, preferred_element_type=jnp.float32
        ).astype(jnp.bfloat16),
        "tp",
    ).astype(jnp.float32)
    residual = features + attended + norm_vectors[2]
    normed_two, norm_two_back = jax.vjp(layer_norm, residual, norm_vectors[3], norm_vectors[4])
    normed_two_low = normed_two.astype(jnp.bfloat16)
    preact = (
        jnp.dot(normed_two_low, gathered_ffn[0], preferred_element_type=jnp.float32) + hidden_bias
    )
    activated, gelu_back = jax.vjp(partial(jax.nn.gelu, approximate=False), preact)
    activated_low = activated.astype(jnp.bfloat16)
    mixed_sum = lax.psum(
        jnp.einsum(
            "tf,df->td", activated_low, gathered_ffn[1], preferred_element_type=jnp.float32
        ).astype(jnp.bfloat16),
        "tp",
    ).astype(jnp.float32)
    layer_output = (residual + mixed_sum + norm_vectors[5]).astype(jnp.bfloat16)
    grad_output = out_grad.astype(jnp.float32)
    grad_down = jnp.einsum("td,tf->df", out_grad, activated_low, preferred_element_type=jnp.float32)
    grad_act = jnp.einsum(
        "td,df->tf", out_grad, gathered_ffn[1], preferred_element_type=jnp.float32
    )
    grad_pre = gelu_back(grad_act)[0].astype(jnp.bfloat16)
    grad_up = jnp.einsum("td,tf->df", normed_two_low, grad_pre, preferred_element_type=jnp.float32)
    grad_hidden_bias = jnp.sum(grad_pre.astype(jnp.float32), axis=0)
    grad_normed_two = lax.psum(
        jnp.einsum(
            "tf,df->td", grad_pre, gathered_ffn[0], preferred_element_type=jnp.float32
        ).astype(jnp.bfloat16),
        "tp",
    ).astype(jnp.float32)
    grad_residual_ln, grad_gain_two, grad_shift_two = norm_two_back(grad_normed_two)
    grad_residual = grad_output + grad_residual_ln
    grad_residual_low = grad_residual.astype(jnp.bfloat16)
    grad_out_projection = jnp.einsum(
        "td,tw->dw", grad_residual_low, heads_low, preferred_element_type=jnp.float32
    )
    grad_heads = jnp.einsum(
        "td,dw->tw", grad_residual_low, out_projection, preferred_element_type=jnp.float32
    )
    grad_heads = grad_heads.astype(jnp.bfloat16).reshape(row_count, slot_count, local_heads, HD)
    grad_turned_q, grad_turned_k, grad_values = lax.map(
        lambda packed: attend_row_back(
            packed[0], packed[1], packed[2], packed[3], packed[4], packed[5], block_rows
        ),
        (turned_low[0], turned_low[1], values_low, segment_ids, log_total, grad_heads),
    )
    grad_shaped_qk = rotate_back(jnp.stack([grad_turned_q, grad_turned_k]))[0]
    grad_projected = jnp.concatenate([grad_shaped_qk, grad_values[None]], axis=0)
    grad_projected = grad_projected.reshape(3, token_count, head_width).astype(jnp.bfloat16)
    grad_head_bias = jnp.sum(grad_projected.astype(jnp.float32), axis=1)
    grad_qkv = jnp.einsum(
        "td,ctw->cdw", normed_low, grad_projected, preferred_element_type=jnp.float32
    )
    grad_normed = lax.psum(
        jnp.einsum(
            "ctw,cdw->td", grad_projected, gathered_attn[:3], preferred_element_type=jnp.float32
        ).astype(jnp.bfloat16),
        "tp",
    ).astype(jnp.float32)
    grad_features_ln, grad_gain, grad_shift = norm_back(grad_normed)
    input_grad = (grad_residual + grad_features_ln).astype(jnp.bfloat16)
    grad_vectors = jnp.stack(
        [
            grad_gain,
            grad_shift,
            jnp.sum(grad_residual, axis=0),
            grad_gain_two,
            grad_shift_two,
            jnp.sum(grad_output, axis=0),
        ]
    )
    grad_attn = jnp.concatenate([grad_qkv, grad_out_projection[None]], axis=0)
    grad_ffn = jnp.stack([grad_up, grad_down])
    full_attn, full_ffn, sum_head, sum_hidden, sum_vectors = lax.psum(
        (grad_attn, grad_ffn, grad_head_bias, grad_hidden_bias, grad_vectors), "dp"
    )
    offset_rows = lax.axis_index("dp") * shard_rows
    own_attn = lax.dynamic_slice_in_dim(full_attn, offset_rows, shard_rows, 1)
    own_ffn = lax.dynamic_slice_in_dim(full_ffn, offset_rows, shard_rows, 1)
    grads_list = [own_attn, own_ffn, sum_head, sum_hidden.reshape(1, -1), sum_vectors]
    firsts = [attn_first, ffn_first, head_first, hidden_first.reshape(1, -1), vector_first]
    seconds = [attn_second, ffn_second, head_second, hidden_second.reshape(1, -1), vector_second]
    results = [
        lamb_moments(masters[member], grads_list[member], firsts[member], seconds[member])
        for member in range(5)
    ]
    update_terms = jnp.concatenate(
        [sum_squares(results[member][2]) * replicas[member] for member in range(5)]
    )
    update_sums = lax.psum(update_terms, ("dp", "tp"))
    weight_norms = jnp.sqrt(weight_sums)
    update_norms = jnp.sqrt(update_sums)
    trust_ratio = weight_norms / update_norms
    counts = [4, 2, 3, 1, 6]
    new_weights = []
    begin_at = 0
    for member in range(5):
        piece_ratio = trust_ratio[begin_at : begin_at + counts[member]]
        shaped_ratio = piece_ratio.reshape((-1,) + (1,) * (masters[member].ndim - 1))
        new_weights.append(masters[member] - RATE * shaped_ratio * results[member][2])
        begin_at += counts[member]
    return (
        layer_output,
        input_grad,
        new_weights[0],
        new_weights[1],
        new_weights[2],
        new_weights[3].reshape(-1),
        new_weights[4],
        results[0][0],
        results[1][0],
        results[2][0],
        results[3][0].reshape(-1),
        results[4][0],
        results[0][1][:3],
        results[0][1][3],
        results[1][1],
        results[2][1],
        results[3][1].reshape(-1),
        results[4][1][2:],
        results[4][1][:2],
        jnp.stack([weight_norms, update_norms]),
    )


def solution(mesh):
    in_specs = (
        P("dp", None),
        P("dp", None),
        P("dp", None),
        P(None, "dp", "tp"),
        P(None, "dp", "tp"),
        P(None, "tp"),
        P("tp"),
        P(),
        P(None, "dp", "tp"),
        P(None, "dp", "tp"),
        P(None, "tp"),
        P("tp"),
        P(),
        P(None, "dp", "tp"),
        P(None, "dp", "tp"),
        P(None, "tp"),
        P("tp"),
        P(),
    )
    out_specs = (
        P("dp", None),
        P("dp", None),
        P(None, "dp", "tp"),
        P(None, "dp", "tp"),
        P(None, "tp"),
        P("tp"),
        P(),
        P(None, "dp", "tp"),
        P(None, "dp", "tp"),
        P(None, "tp"),
        P("tp"),
        P(),
        P(None, "dp", "tp"),
        P("dp", "tp"),
        P(None, "dp", "tp"),
        P(None, "tp"),
        P("tp"),
        P(),
        P(),
        P(),
    )
    return jax.shard_map(
        on_device, mesh=mesh, in_specs=in_specs, out_specs=out_specs, check_vma=False
    )
```

profile of v0, /device:TPU:12, one launch (start us, length us, event | category | flops | bytes accessed | tf_op | source)
XLA Modules:
  0.0 1304.4 jit_solution(11081138493760027001)
XLA Ops:
  17.8 34.1 %all-gather.3.cloned.1.call-done = bf16[4,640,320]{2,0,1:T(4,128)(2,1)} async-done(((bf16[4,40,320]{2,0,1:T(4,128)(2,1)}), bf16[4,640,320]{2,0,1:T(4,128)(2,1)}) %all-gather.3.cloned.1.call-update) | async-done | bytes 1638416 | tf_op jit(solution)/shard_map/all_gather | solution.py:164
  67.5 8.1 slice.89
  88.0 138.8 %while.54 = (s32[]{:T(128)}, bf16[2,1024,10,32]{3,2,1,0:T(8,128)(2,1)}, f32[2,2,10,512]{3,2,1,0:T(8,128)}, bf16[2,1024,10,32]{1,3,2,0:T(8,128)(2,1)S(1)}, s32[2,...) while((s32[]{:T(128)}, ...), condition=%wide.region_8.0_spmd, body=%wide.region_3.8_spmd.sunk | while | flops 734522368 | bytes 181594624 | solution.py:181
  92.8 54.8 %while.57 = (s32[]{:T(128)}, bf16[2,512,10,32]{1,3,2,0:T(8,128)(2,1)S(1)}, f32[2,10,512]{2,1,0:T(8,128)S(1)}, s32[2,512]{1,0:T(2,128)S(1)}, s32[1024]{0:T(1024)S...) while((s32[]{:T(128)}, ...), condition=%wide.region_7.7_spmd, body=%wide.region_4.6_spmd.sunk | while | flops 734522368 | bytes 154048688 | solution.py:92
  110.5 9.7 fusion.157
  137.9 9.7 fusion.157
  162.2 54.8 %while.57 = (s32[]{:T(128)}, bf16[2,512,10,32]{1,3,2,0:T(8,128)(2,1)S(1)}, f32[2,10,512]{2,1,0:T(8,128)S(1)}, s32[2,512]{1,0:T(2,128)S(1)}, s32[1024]{0:T(1024)S...) while((s32[]{:T(128)}, ...), condition=%wide.region_7.7_spmd, body=%wide.region_4.6_spmd.sunk | while | flops 734522368 | bytes 154048688 | solution.py:92
  179.8 9.7 fusion.157
  207.2 9.7 fusion.157
  227.8 10.1 reshape.337
  243.5 72.7 %all-reduce.11.cloned.1.call-done = bf16[2048,640]{1,0:T(8,128)(2,1)} async-done(((bf16[2048,640]{1,0:T(8,128)(2,1)}), bf16[2048,640]{1,0:T(8,128)(2,1)}) %all-reduce.11.cloned.1.call-update) | async-done | bytes 2621456 | tf_op jit(solution)/shard_map/psum | solution.py:187
  320.5 46.1 %all-gather.5.cloned.1.call-done = bf16[2,640,1280]{2,1,0:T(8,128)(2,1)} async-done(((bf16[2,40,1280]{2,1,0:T(8,128)(2,1)}), bf16[2,640,1280]{2,1,0:T(8,128)(2,1)}) %all-gather.5.cloned.1.call-update) | async-done | bytes 3276816 | tf_op jit(solution)/shard_map/all_gather | solution.py:165
  366.6 31.1 %multiply_convert_fusion.1 = (bf16[2048,1280]{1,0:T(8,128)(2,1)}, f32[2048,1280]{1,0:T(8,128)}, f32[2048,1280]{1,0:T(8,128)}) fusion(f32[1280]{0:T(1024)S(1)} %copy-done.50, bf16[2,640,1280]{2,1,0:T(8,128)(2,1)} %all-gather.5.cloned.1.call-done, f32[640]{0:T(1024)S(1)} %copy-done.58, f32[640]{0:T(1024)S(1)} %copy-done.47, f32[2048]{0:T(1024)S(1)} %fusion.84, ...), kind=kOutput, calls=%fused_computation.69 | convolution fusion | flops 3540254720 | bytes 33124864 | tf_op jit(solution)/shard_map/dot_general | solution.py:197
  397.8 12.4 convert_reduce_fusion
  433.5 56.9 %all-reduce.13.cloned.1.call-done = bf16[2048,640]{1,0:T(8,128)(2,1)} async-done(((bf16[2048,640]{1,0:T(8,128)(2,1)}), bf16[2048,640]{1,0:T(8,128)(2,1)}) %all-reduce.13.cloned.1.call-update) | async-done | bytes 2621456 | tf_op jit(solution)/shard_map/psum | solution.py:216
  510.4 277.2 %while.56 = (s32[]{:T(128)}, f32[2,1024,10,32]{1,3,2,0:T(8,128)}, f32[2,1024,10,32]{1,3,2,0:T(8,128)}, bf16[2,1024,10,32]{1,3,2,0:T(8,128)(2,1)}, bf16[2,1024,10...) while((s32[]{:T(128)}, f32[2,1024,10,32]{1,3,2,0:T(8,128)}, ...), condition=%wide.region_20.21_spmd, body=%wide.region_16.20_spmd.sunk | while | flops 1758686208 | bytes 284158464 | solution.py:232
  522.2 111.2 %while.58 = (s32[]{:T(128)}, f32[1024,10,32]{0,2,1:T(8,128)S(1)}, f32[1024,10,32]{0,2,1:T(8,128)}, f32[2,512,10,32]{1,3,2,0:T(8,128)}, bf16[2,512,10,32]{1,3,2,0...) while((s32[]{:T(128)}, f32[1024,10,32]{0,2,1:T(8,128)S(1)}, ...), condition=%wide.region_19.19_spmd.clone, body=%wide.region_17.18_spmd.clone.sunk | while | flops 1758686208 | bytes 255219920 | solution.py:110
  541.9 15.2 %multiply_reduce_fusion.13 = (f32[10,512]{1,0:T(8,128)S(1)}, f32[10,512,1024]{2,1,0:T(8,128)}) fusion(f32[10,512,1024]{2,1,0:T(8,128)} %copy-done, f32[10,512]{1,0:T(8,128)S(1)} %dynamic-slice_bitcast_fusion.15, pred[512,1024]{1,0:T(8,128)(4,1)S(1)} %broadcast_compare_fusion.4, bf16[1024,10,32]{0,2,1:T(8,128)(2,1)} %get-tuple-element.1035, ...), kind=kOutput, calls=%fused_computation.18.clone.1 | convolution fusion | flops 361753600 | bytes 43491332 | tf_op jit(solution)/shard_map/while/body/eval_jaxpr/while/body/eval_jaxpr/qhd,khd->hqk/dot_general | solution.py:69
  557.0 14.6 %multiply_convert_fusion.3 = bf16[10,512,1024]{2,1,0:T(8,128)(2,1)S(1)} fusion(f32[10,512,1024]{2,1,0:T(8,128)} %get-tuple-element.987, f32[10,512,1024]{2,1,0:T(8,128)} %copy-done, f32[10,512]{1,0:T(8,128)S(1)} %get-tuple-element.988, f32[10,512]{1,0:T(8,128)S(1)} %dynamic-slice_bitcast_fusion.15, pred[512,1024]{1,0:T(8,128)(4,1)S(1)} %broadcast_compare_fusion.4), kind=kLoop, calls=%fused_computation.17.clone.1 | loop fusion | flops 31457280 | bytes 52994048 | tf_op jit(solution)/shard_map/while/body/eval_jaxpr/while/body/eval_jaxpr/convert_element_type | solution.py:73
  597.6 15.2 %multiply_reduce_fusion.13 = (f32[10,512]{1,0:T(8,128)S(1)}, f32[10,512,1024]{2,1,0:T(8,128)}) fusion(f32[10,512,1024]{2,1,0:T(8,128)} %copy-done, f32[10,512]{1,0:T(8,128)S(1)} %dynamic-slice_bitcast_fusion.15, pred[512,1024]{1,0:T(8,128)(4,1)S(1)} %broadcast_compare_fusion.4, bf16[1024,10,32]{0,2,1:T(8,128)(2,1)} %get-tuple-element.1035, ...), kind=kOutput, calls=%fused_computation.18.clone.1 | convolution fusion | flops 361753600 | bytes 43491332 | tf_op jit(solution)/shard_map/while/body/eval_jaxpr/while/body/eval_jaxpr/qhd,khd->hqk/dot_general | solution.py:69
  612.8 14.6 %multiply_convert_fusion.3 = bf16[10,512,1024]{2,1,0:T(8,128)(2,1)S(1)} fusion(f32[10,512,1024]{2,1,0:T(8,128)} %get-tuple-element.987, f32[10,512,1024]{2,1,0:T(8,128)} %copy-done, f32[10,512]{1,0:T(8,128)S(1)} %get-tuple-element.988, f32[10,512]{1,0:T(8,128)S(1)} %dynamic-slice_bitcast_fusion.15, pred[512,1024]{1,0:T(8,128)(4,1)S(1)} %broadcast_compare_fusion.4), kind=kLoop, calls=%fused_computation.17.clone.1 | loop fusion | flops 31457280 | bytes 52994048 | tf_op jit(solution)/shard_map/while/body/eval_jaxpr/while/body/eval_jaxpr/convert_element_type | solution.py:73
  660.5 111.2 %while.58 = (s32[]{:T(128)}, f32[1024,10,32]{0,2,1:T(8,128)S(1)}, f32[1024,10,32]{0,2,1:T(8,128)}, f32[2,512,10,32]{1,3,2,0:T(8,128)}, bf16[2,512,10,32]{1,3,2,0...) while((s32[]{:T(128)}, f32[1024,10,32]{0,2,1:T(8,128)S(1)}, ...), condition=%wide.region_19.19_spmd.clone, body=%wide.region_17.18_spmd.clone.sunk | while | flops 1758686208 | bytes 255219920 | solution.py:110
  680.2 15.2 %multiply_reduce_fusion.13 = (f32[10,512]{1,0:T(8,128)S(1)}, f32[10,512,1024]{2,1,0:T(8,128)}) fusion(f32[10,512,1024]{2,1,0:T(8,128)} %copy-done, f32[10,512]{1,0:T(8,128)S(1)} %dynamic-slice_bitcast_fusion.15, pred[512,1024]{1,0:T(8,128)(4,1)S(1)} %broadcast_compare_fusion.4, bf16[1024,10,32]{0,2,1:T(8,128)(2,1)} %get-tuple-element.1035, ...), kind=kOutput, calls=%fused_computation.18.clone.1 | convolution fusion | flops 361753600 | bytes 43491332 | tf_op jit(solution)/shard_map/while/body/eval_jaxpr/while/body/eval_jaxpr/qhd,khd->hqk/dot_general | solution.py:69
  695.3 14.6 %multiply_convert_fusion.3 = bf16[10,512,1024]{2,1,0:T(8,128)(2,1)S(1)} fusion(f32[10,512,1024]{2,1,0:T(8,128)} %get-tuple-element.987, f32[10,512,1024]{2,1,0:T(8,128)} %copy-done, f32[10,512]{1,0:T(8,128)S(1)} %get-tuple-element.988, f32[10,512]{1,0:T(8,128)S(1)} %dynamic-slice_bitcast_fusion.15, pred[512,1024]{1,0:T(8,128)(4,1)S(1)} %broadcast_compare_fusion.4), kind=kLoop, calls=%fused_computation.17.clone.1 | loop fusion | flops 31457280 | bytes 52994048 | tf_op jit(solution)/shard_map/while/body/eval_jaxpr/while/body/eval_jaxpr/convert_element_type | solution.py:73
  735.9 15.2 %multiply_reduce_fusion.13 = (f32[10,512]{1,0:T(8,128)S(1)}, f32[10,512,1024]{2,1,0:T(8,128)}) fusion(f32[10,512,1024]{2,1,0:T(8,128)} %copy-done, f32[10,512]{1,0:T(8,128)S(1)} %dynamic-slice_bitcast_fusion.15, pred[512,1024]{1,0:T(8,128)(4,1)S(1)} %broadcast_compare_fusion.4, bf16[1024,10,32]{0,2,1:T(8,128)(2,1)} %get-tuple-element.1035, ...), kind=kOutput, calls=%fused_computation.18.clone.1 | convolution fusion | flops 361753600 | bytes 43491332 | tf_op jit(solution)/shard_map/while/body/eval_jaxpr/while/body/eval_jaxpr/qhd,khd->hqk/dot_general | solution.py:69
  751.1 14.6 %multiply_convert_fusion.3 = bf16[10,512,1024]{2,1,0:T(8,128)(2,1)S(1)} fusion(f32[10,512,1024]{2,1,0:T(8,128)} %get-tuple-element.987, f32[10,512,1024]{2,1,0:T(8,128)} %copy-done, f32[10,512]{1,0:T(8,128)S(1)} %get-tuple-element.988, f32[10,512]{1,0:T(8,128)S(1)} %dynamic-slice_bitcast_fusion.15, pred[512,1024]{1,0:T(8,128)(4,1)S(1)} %broadcast_compare_fusion.4), kind=kLoop, calls=%fused_computation.17.clone.1 | loop fusion | flops 31457280 | bytes 52994048 | tf_op jit(solution)/shard_map/while/body/eval_jaxpr/while/body/eval_jaxpr/convert_element_type | solution.py:73
  817.2 8.9 convolution_convert_fusion.1
  837.5 182.1 %all-reduce.15.cloned.1.call-done = (f32[4,640,320]{2,1,0:T(8,128)}, f32[2,640,1280]{2,1,0:T(8,128)}) async-done(((f32[4,640,320]{2,1,0:T(8,128)}, f32[2,640,1280]{2,1,0:T(8,128)}), (f32[4,640,320]{2,1,0:T(8,128)}, f32[2,640,1280]{2,1,0:T(8,128)})) %all-reduce.15.cloned.1.call-update) | async-done | bytes 9830416 | tf_op jit(solution)/shard_map/psum | solution.py:265
  1025.9 126.9 %all-reduce.17.cloned.1.call-done = (bf16[2048,640]{1,0:T(8,128)(2,1)}, bf16[2048,640]{1,0:T(8,128)(2,1)}) async-done(((bf16[2048,640]{1,0:T(8,128)(2,1)}, bf16[2048,640]{1,0:T(8,128)(2,1)}), (bf16[2048,640]{1,0:T(8,128)(2,1)}, bf16[2048,640]{1,0:T(8,128)(2,1)})) %all-reduce.17.cloned.1.call-update) | async-done | bytes 5242896 | tf_op jit(solution)/shard_map/psum | solution.py:201
  1161.9 54.0 %all-reduce.3 = (f32[3,320]{1,0:T(4,128)}, f32[1280]{0:T(1024)}, f32[6,640]{1,0:T(8,128)}) all-reduce(f32[3,320]{1,0:T(4,128)} %convert_reduce_fusion.2, f32[1280]{0:T(1024)} %get-tuple-element.699, f32[6,640]{1,0:T(8,128)S(1)} %stack.48), channel_id=1, replica_groups=mesh['dp'=16,'tp'=2] {'dp'}, use_global_device_ids=true, to_apply=%region_35.36 | all-reduce | flops 6080 | bytes 48640 | tf_op jit(solution)/shard_map/psum | solution.py:265
  1226.4 48.9 %all-reduce.2 = (f32[16]{0:T(128)}, f32[16]{0:T(128)}) all-reduce(f32[16]{0:T(128)} %concatenate.39, f32[16]{0:T(128)} %concatenate.37), channel_id=1, replica_groups=mesh['dp'=16,'tp'=2] {'dp','tp'}, use_global_device_ids=true, to_apply=%region_48.49 | all-reduce | flops 32 | bytes 256 | tf_op jit(solution)/shard_map/psum | solution.py:281
  1288.0 9.4 add_convert_fusion.1
  (381 shorter events, 426.6 us)
Async XLA Ops:
  7.2 49.2 %copy-start.51 = (f32[3,320]{1,0:T(4,128)S(1)}, f32[3,320]{1,0:T(4,128)}, u32[]{:S(2)}) copy-start(f32[3,320]{1,0:T(4,128)} %param.31) | copy-start | bytes 11524
  7.2 44.7 %all-gather.3.cloned.1.call-start = ((), (), s32[]{:S(2)}) async-start(), calls=%async_computation | async-start | bytes 2088960 | tf_op jit(solution)/shard_map/all_gather | solution.py:164
  9.1 307.1 %all-reduce.11.cloned.1.call-start = ((), (), s32[]{:S(2)}) async-start(), calls=%async_computation.1 | async-start | bytes 5242880 | tf_op jit(solution)/shard_map/psum | solution.py:187
  10.8 50.4 %copy-start.48 = (f32[640]{0:T(1024)}, f32[640]{0:T(1024)S(1)}, u32[]{:S(2)}) copy-start(f32[640]{0:T(1024)S(1)} %get-tuple-element.571) | copy-start | bytes 7684
  10.8 50.4 %copy-start.56 = (f32[640]{0:T(1024)}, f32[640]{0:T(1024)S(1)}, u32[]{:S(2)}) copy-start(f32[640]{0:T(1024)S(1)} %get-tuple-element.570) | copy-start | bytes 7684
  13.8 69.5 %copy-start.29 = (f32[2,1024,32]{1,2,0:T(8,128)}, f32[2,1024,32]{1,2,0:T(8,128)S(1)}, u32[]{:S(2)}) copy-start(f32[2,1024,32]{1,2,0:T(8,128)S(1)} %get-tuple-element.692) | copy-start | bytes 786436
  13.8 69.5 %copy-start.31 = (f32[2,1024,32]{1,2,0:T(8,128)}, f32[2,1024,32]{1,2,0:T(8,128)S(1)}, u32[]{:S(2)}) copy-start(f32[2,1024,32]{1,2,0:T(8,128)S(1)} %get-tuple-element.693) | copy-start | bytes 786436
  16.2 45.1 %copy-start.38 = (f32[2048]{0:T(1024)}, f32[2048]{0:T(1024)S(1)}, u32[]{:S(2)}) copy-start(f32[2048]{0:T(1024)S(1)} %broadcast_multiply_fusion.2) | copy-start | bytes 24580
  17.8 43.4 %copy-start.43 = (f32[2048]{0:T(1024)}, f32[2048]{0:T(1024)S(1)}, u32[]{:S(2)}) copy-start(f32[2048]{0:T(1024)S(1)} %fusion.83) | copy-start | bytes 24580
  92.8 54.8 %copy-start.36 = (f32[2,2,10,512]{3,2,1,0:T(8,128)S(1)}, f32[2,2,10,512]{3,2,1,0:T(8,128)}, u32[]{:S(2)}) copy-start(f32[2,2,10,512]{3,2,1,0:T(8,128)} %get-tuple-element.1077) | copy-start | bytes 245764 | tf_op jit(solution)/shard_map/while
  162.2 54.8 %copy-start.36 = (f32[2,2,10,512]{3,2,1,0:T(8,128)S(1)}, f32[2,2,10,512]{3,2,1,0:T(8,128)}, u32[]{:S(2)}) copy-start(f32[2,2,10,512]{3,2,1,0:T(8,128)} %get-tuple-element.1077) | copy-start | bytes 245764 | tf_op jit(solution)/shard_map/while
  217.0 9.7 copy-start.37
  226.8 11.1 copy-start.34
  237.9 78.3 %copy-start.4 = (bf16[2048,640]{1,0:T(8,128)(2,1)S(1)}, bf16[2048,640]{1,0:T(8,128)(2,1)}, u32[]{:S(2)}) copy-start(bf16[2048,640]{1,0:T(8,128)(2,1)} %param.26) | copy-start | bytes 7864324
  237.9 78.3 %copy-start.40 = (f32[640]{0:T(1024)S(1)}, f32[640]{0:T(1024)}, u32[]{:S(2)}) copy-start(f32[640]{0:T(1024)} %get-tuple-element.569) | copy-start | bytes 7684
  242.7 123.9 %all-gather.5.cloned.1.call-start = ((), (), s32[]{:S(2)}) async-start(), calls=%async_computation.2 | async-start | bytes 3481600 | tf_op jit(solution)/shard_map/all_gather | solution.py:165
  243.4 247.0 %all-reduce.13.cloned.1.call-start = ((), (), s32[]{:S(2)}) async-start(), calls=%async_computation.3 | async-start | bytes 5242880 | tf_op jit(solution)/shard_map/psum | solution.py:216
  316.2 50.4 %copy-start.47 = (f32[640]{0:T(1024)S(1)}, f32[640]{0:T(1024)}, u32[]{:S(2)}) copy-start(f32[640]{0:T(1024)} %get-tuple-element.568) | copy-start | bytes 7684
  316.2 50.4 %copy-start.50 = (f32[1280]{0:T(1024)S(1)}, f32[1280]{0:T(1024)}, u32[]{:S(2)}) copy-start(f32[1280]{0:T(1024)} %param.32) | copy-start | bytes 15364
  316.2 50.4 %copy-start.58 = (f32[640]{0:T(1024)S(1)}, f32[640]{0:T(1024)}, u32[]{:S(2)}) copy-start(f32[640]{0:T(1024)} %get-tuple-element.567) | copy-start | bytes 7684
  366.6 31.1 %copy-start.27 = (bf16[2048,640]{1,0:T(8,128)(2,1)S(1)}, bf16[2048,640]{1,0:T(8,128)(2,1)}, u32[]{:S(2)}) copy-start(bf16[2048,640]{1,0:T(8,128)(2,1)} %param.27) | copy-start | bytes 7864324
  366.6 31.1 %copy-start.59 = (bf16[2,640,1280]{2,1,0:T(8,128)(2,1)S(1)}, bf16[2,640,1280]{2,1,0:T(8,128)(2,1)}, u32[]{:S(2)}) copy-start(bf16[2,640,1280]{2,1,0:T(8,128)(2,1)} %all-gather.5.cloned.1.call-done) | copy-start | bytes 9830404
  418.5 601.2 %all-reduce.15.cloned.1.call-start = ((), (), s32[]{:S(2)}) async-start(), calls=%async_computation.4 | async-start | bytes 20971520 | tf_op jit(solution)/shard_map/psum | solution.py:265
  557.0 14.6 %copy-start.2 = (bf16[2,512,10,32]{1,3,2,0:T(8,128)(2,1)S(1)}, bf16[2,512,10,32]{1,3,2,0:T(8,128)(2,1)}, u32[]{:S(2)}) copy-start(bf16[2,512,10,32]{1,3,2,0:T(8,128)(2,1)} %get-tuple-element.1029) | copy-start | bytes 1966084 | tf_op jit(solution)/shard_map/while/body/eval_jaxpr/while
  612.8 14.6 %copy-start.2 = (bf16[2,512,10,32]{1,3,2,0:T(8,128)(2,1)S(1)}, bf16[2,512,10,32]{1,3,2,0:T(8,128)(2,1)}, u32[]{:S(2)}) copy-start(bf16[2,512,10,32]{1,3,2,0:T(8,128)(2,1)} %get-tuple-element.1029) | copy-start | bytes 1966084 | tf_op jit(solution)/shard_map/while/body/eval_jaxpr/while
  695.3 14.6 %copy-start.2 = (bf16[2,512,10,32]{1,3,2,0:T(8,128)(2,1)S(1)}, bf16[2,512,10,32]{1,3,2,0:T(8,128)(2,1)}, u32[]{:S(2)}) copy-start(bf16[2,512,10,32]{1,3,2,0:T(8,128)(2,1)} %get-tuple-element.1029) | copy-start | bytes 1966084 | tf_op jit(solution)/shard_map/while/body/eval_jaxpr/while
  751.1 14.6 %copy-start.2 = (bf16[2,512,10,32]{1,3,2,0:T(8,128)(2,1)S(1)}, bf16[2,512,10,32]{1,3,2,0:T(8,128)(2,1)}, u32[]{:S(2)}) copy-start(bf16[2,512,10,32]{1,3,2,0:T(8,128)(2,1)} %get-tuple-element.1029) | copy-start | bytes 1966084 | tf_op jit(solution)/shard_map/while/body/eval_jaxpr/while
  817.1 335.7 %all-reduce.17.cloned.1.call-start = ((), (), s32[]{:S(2)}) async-start(), calls=%async_computation.5 | async-start | bytes 10485760 | tf_op jit(solution)/shard_map/psum | solution.py:201
  831.1 188.6 %copy-start.33 = (f32[4,40,320]{2,1,0:T(8,128)S(1)}, f32[4,40,320]{2,1,0:T(8,128)}, u32[]{:S(2)}) copy-start(f32[4,40,320]{2,1,0:T(8,128)} %param.29) | copy-start | bytes 614404
  831.1 191.8 %copy-start.26 = (f32[2,40,1280]{2,1,0:T(8,128)S(1)}, f32[2,40,1280]{2,1,0:T(8,128)}, u32[]{:S(2)}) copy-start(f32[2,40,1280]{2,1,0:T(8,128)} %param.30) | copy-start | bytes 1228804
  837.5 319.3 %copy-start.46 = (f32[2048]{0:T(1024)S(1)}, f32[2048]{0:T(1024)}, u32[]{:S(2)}) copy-start(f32[2048]{0:T(1024)} %copy-done.45) | copy-start | bytes 24580
  1156.2 131.7 %copy-start.41 = (f32[640]{0:T(1024)S(1)}, f32[640]{0:T(1024)}, u32[]{:S(2)}) copy-start(f32[640]{0:T(1024)} %get-tuple-element.569) | copy-start | bytes 7684
  (55 other events, 259.5 us)
Sparse Core Ops, SparseCore 0:
  10.9 40.9 all-gather.2
  242.8 73.3 all-reduce.10
  319.2 47.3 all-gather.4
  418.6 71.8 all-reduce.12
  817.2 202.3 all-reduce.14
  1022.7 130.0 all-reduce.16
where the time goes:
time: 1320 us; the launch traced here: 1300 us
  waiting for transfers between devices  519 us (39%)
  matrix products  279 us (21%)
  local copies, waits for them, and re-layouts  218 us (17%)
  other arithmetic  167 us (13%)
  blocking collectives  103 us (8%)
  between operations  17 us (1%)
    psum x1, waiting for transfers between devices, on_device(): lax.psum((grad_attn, grad_ffn, grad_head_bias, grad_hidden_bias, grad_vec...  182 us
    psum x1, waiting for transfers between devices, on_device(): lax.psum(jnp.einsum('tf,df->td', activated_low, gathered_ffn[1], preferre...  127 us
    psum x1, waiting for transfers between devices, on_device(): lax.psum(jnp.einsum('tw,dw->td', heads_low, out_projection, preferred_ele...  72.7 us
    dot_general x4, matrix products, attend_block_back(): jnp.einsum('qhd,khd->hqk', grad_heads, values_row, preferred_element_type...  60.6 us
    while x56, local copies, waits for them, and re-layouts  59.7 us
    convert_element_type x4, other arithmetic, attend_block_back(): grad_scores = (attention * (grad_attention - center)).astype(jnp.bfloat16)  58.3 us
    psum x1, waiting for transfers between devices, on_device(): lax.psum(jnp.einsum('tf,df->td', grad_pre, gathered_ffn[0], preferred_ele...  56.9 us
    psum x1, blocking collectives, on_device(): lax.psum((grad_attn, grad_ffn, grad_head_bias, grad_hidden_bias, grad_vec...  54 us
  transfers between devices with their start and end apart: 6, of which 6 were waited for; matrix products, arithmetic and copies ran while one was open for 4% of the time, Pallas kernels for 0%

commit v1 on v0

--- a/solution.py
+++ b/solution.py
@@ -198,11 +198,11 @@
     )
     activated, gelu_back = jax.vjp(partial(jax.nn.gelu, approximate=False), preact)
     activated_low = activated.astype(jnp.bfloat16)
-    mixed_sum = lax.psum(
+    plan_numbers = lambda buf: lax.all_gather(buf, "tp").sum(axis=0)
+    mixed_sum = plan_numbers(
         jnp.einsum(
             "tf,df->td", activated_low, gathered_ffn[1], preferred_element_type=jnp.float32
-        ).astype(jnp.bfloat16),
-        "tp",
+        ).astype(jnp.bfloat16)
     ).astype(jnp.float32)
     layer_output = (residual + mixed_sum + norm_vectors[5]).astype(jnp.bfloat16)
     grad_output = out_grad.astype(jnp.float32)

time: 1320 us -> 1240 us (0.939)
  waiting for transfers between devices: 519 us -> 449 us
    psum x1, waiting for transfers between devices: 127 us -> 48.7 us  [on_device(): lax.psum(jnp.einsum('ctw,cdw->td', grad_projected, gathered_attn[:3], pre...]
    all_gather x0 -> x1, waiting for transfers between devices: none -> 60.7 us  [on_device(): plan_numbers = lambda buf: lax.all_gather(buf, 'tp').sum(axis=0)]
    psum x1, waiting for transfers between devices: 182 us -> 133 us  [on_device(): lax.psum((grad_attn, grad_ffn, grad_head_bias, grad_hidden_bias, grad_vec...]
  transfers between devices with their start and end apart: 6 -> 7, of which waited for: 6 -> 7; matrix products, arithmetic and copies ran while one was open for 4% -> 7% of each run, Pallas kernels for 0% -> 0%
where the time goes in v1:
time: 1240 us; the launch traced here: 1230 us
  waiting for transfers between devices  449 us (36%)
  matrix products  286 us (23%)
  local copies, waits for them, and re-layouts  217 us (18%)
  other arithmetic  163 us (13%)
  blocking collectives  96.2 us (8%)
  between operations  17.4 us (1%)
    psum x1, waiting for transfers between devices, on_device(): lax.psum((grad_attn, grad_ffn, grad_head_bias, grad_hidden_bias, grad_vec...  133 us
    psum x1, waiting for transfers between devices, on_device(): lax.psum(jnp.einsum('tw,dw->td', heads_low, out_projection, preferred_ele...  72.7 us
    all_gather x1, waiting for transfers between devices, on_device(): plan_numbers = lambda buf: lax.all_gather(buf, 'tp').sum(axis=0)  60.7 us
    dot_general x4, matrix products, attend_block_back(): jnp.einsum('qhd,khd->hqk', grad_heads, values_row, preferred_element_type...  60.7 us
    while x56, local copies, waits for them, and re-layouts  59.6 us
    convert_element_type x4, other arithmetic, attend_block_back(): grad_scores = (attention * (grad_attention - center)).astype(jnp.bfloat16)  58.3 us
    psum x1, blocking collectives, on_device(): lax.psum((grad_attn, grad_ffn, grad_head_bias, grad_hidden_bias, grad_vec...  56.1 us
    psum x1, waiting for transfers between devices, on_device(): lax.psum(jnp.einsum('tf,df->td', grad_pre, gathered_ffn[0], preferred_ele...  54 us
  transfers between devices with their start and end apart: 7, of which 7 were waited for; matrix products, arithmetic and copies ran while one was open for 7% of the time, Pallas kernels for 0%

profile of v1, /device:TPU:12, one launch (start us, length us, event | category | flops | bytes accessed | tf_op | source)
XLA Modules:
  0.0 1230.3 jit_solution(10765206592842855156)
XLA Ops:
  17.8 34.1 %all-gather.5.cloned.1.call-done = bf16[4,640,320]{2,0,1:T(4,128)(2,1)} async-done(((bf16[4,40,320]{2,0,1:T(4,128)(2,1)}), bf16[4,640,320]{2,0,1:T(4,128)(2,1)}) %all-gather.5.cloned.1.call-update) | async-done | bytes 1638416 | tf_op jit(solution)/shard_map/all_gather | solution.py:164
  87.7 138.7 %while.54 = (s32[]{:T(128)}, bf16[2,1024,10,32]{3,2,1,0:T(8,128)(2,1)}, f32[2,2,10,512]{3,2,1,0:T(8,128)}, bf16[2,1024,10,32]{1,3,2,0:T(8,128)(2,1)S(1)}, s32[2,...) while((s32[]{:T(128)}, ...), condition=%wide.region_8.0_spmd, body=%wide.region_3.8_spmd.sunk | while | flops 734522368 | bytes 181594624 | solution.py:181
  92.6 54.8 %while.57 = (s32[]{:T(128)}, bf16[2,512,10,32]{1,3,2,0:T(8,128)(2,1)S(1)}, f32[2,10,512]{2,1,0:T(8,128)S(1)}, s32[2,512]{1,0:T(2,128)S(1)}, s32[1024]{0:T(1024)S...) while((s32[]{:T(128)}, ...), condition=%wide.region_7.7_spmd, body=%wide.region_4.6_spmd.sunk | while | flops 734522368 | bytes 154048688 | solution.py:92
  110.2 9.7 fusion.157
  137.6 9.7 fusion.157
  161.9 54.8 %while.57 = (s32[]{:T(128)}, bf16[2,512,10,32]{1,3,2,0:T(8,128)(2,1)S(1)}, f32[2,10,512]{2,1,0:T(8,128)S(1)}, s32[2,512]{1,0:T(2,128)S(1)}, s32[1024]{0:T(1024)S...) while((s32[]{:T(128)}, ...), condition=%wide.region_7.7_spmd, body=%wide.region_4.6_spmd.sunk | while | flops 734522368 | bytes 154048688 | solution.py:92
  179.5 9.7 fusion.157
  206.9 9.7 fusion.157
  227.5 10.3 reshape.338
  243.4 72.7 %all-reduce.10.cloned.1.call-done = bf16[2048,640]{1,0:T(8,128)(2,1)} async-done(((bf16[2048,640]{1,0:T(8,128)(2,1)}), bf16[2048,640]{1,0:T(8,128)(2,1)}) %all-reduce.10.cloned.1.call-update) | async-done | bytes 2621456 | tf_op jit(solution)/shard_map/psum | solution.py:187
  320.4 46.1 %all-gather.7.cloned.1.call-done = bf16[2,640,1280]{2,1,0:T(8,128)(2,1)} async-done(((bf16[2,40,1280]{2,1,0:T(8,128)(2,1)}), bf16[2,640,1280]{2,1,0:T(8,128)(2,1)}) %all-gather.7.cloned.1.call-update) | async-done | bytes 3276816 | tf_op jit(solution)/shard_map/all_gather | solution.py:165
  366.5 31.2 %multiply_convert_fusion.1 = (bf16[2048,1280]{1,0:T(8,128)(2,1)}, f32[2048,1280]{1,0:T(8,128)}, f32[2048,1280]{1,0:T(8,128)}) fusion(f32[1280]{0:T(1024)S(1)} %copy-done.52, bf16[2,640,1280]{2,1,0:T(8,128)(2,1)} %all-gather.7.cloned.1.call-done, f32[640]{0:T(1024)S(1)} %copy-done.73, f32[640]{0:T(1024)S(1)} %copy-done.51, f32[2048]{0:T(1024)S(1)} %fusion.84, ...), kind=kOutput, calls=%fused_computation.69 | convolution fusion | flops 3540254720 | bytes 33124864 | tf_op jit(solution)/shard_map/dot_general | solution.py:197
  397.8 12.4 %convert_reduce_fusion = (f32[1280]{0:T(1024)}, bf16[2048,1280]{1,0:T(8,128)(2,1)S(1)}) fusion(f32[2048,1280]{1,0:T(8,128)} %get-tuple-element.672, bf16[2048,640]{1,0:T(8,128)(2,1)S(1)} %copy-done.26, bf16[2,640,1280]{2,1,0:T(8,128)(2,1)S(1)} %copy-done.74, f32[2048,1280]{1,0:T(8,128)} %get-tuple-element.695, f32[1280]{0:T(1024)S(1)} %copy-done.52), kind=kOutput, calls=%fused_computation.67 | convolution fusion | flops 3400006400 | bytes 30487552 | tf_op jit(solution)/shard_map/td,df->tf/dot_general | solution.py:210
  418.3 8.8 convolution_convert_fusion.1
  427.2 9.0 convolution_bitcast_fusion.1
  436.2 54.0 %all-reduce.12.cloned.1.call-done = bf16[2048,640]{1,0:T(8,128)(2,1)} async-done(((bf16[2048,640]{1,0:T(8,128)(2,1)}), bf16[2048,640]{1,0:T(8,128)(2,1)}) %all-reduce.12.cloned.1.call-update) | async-done | bytes 2621456 | tf_op jit(solution)/shard_map/psum | solution.py:216
  500.1 60.7 %all-gather.9.cloned.1.call-done = bf16[4096,640]{1,0:T(8,128)(2,1)} async-done(((bf16[2048,640]{1,0:T(8,128)(2,1)}), bf16[4096,640]{1,0:T(8,128)(2,1)}) %all-gather.9.cloned.1.call-update) | async-done | bytes 5242896 | tf_op jit(solution)/shard_map/all_gather | solution.py:201
  580.6 277.4 %while.56 = (s32[]{:T(128)}, f32[2,1024,10,32]{1,3,2,0:T(8,128)}, f32[2,1024,10,32]{1,3,2,0:T(8,128)}, bf16[2,1024,10,32]{1,3,2,0:T(8,128)(2,1)}, bf16[2,1024,10...) while((s32[]{:T(128)}, f32[2,1024,10,32]{1,3,2,0:T(8,128)}, ...), condition=%wide.region_20.21_spmd, body=%wide.region_16.20_spmd.sunk | while | flops 1758686208 | bytes 284158464 | solution.py:232
  592.6 111.3 %while.58 = (s32[]{:T(128)}, f32[1024,10,32]{0,2,1:T(8,128)S(1)}, f32[1024,10,32]{0,2,1:T(8,128)}, f32[2,512,10,32]{1,3,2,0:T(8,128)}, bf16[2,512,10,32]{1,3,2,0...) while((s32[]{:T(128)}, f32[1024,10,32]{0,2,1:T(8,128)S(1)}, ...), condition=%wide.region_19.19_spmd.clone, body=%wide.region_17.18_spmd.clone.sunk | while | flops 1758686208 | bytes 255219920 | solution.py:110
  612.3 15.2 %multiply_reduce_fusion.13 = (f32[10,512]{1,0:T(8,128)S(1)}, f32[10,512,1024]{2,1,0:T(8,128)}) fusion(f32[10,512,1024]{2,1,0:T(8,128)} %copy-done, f32[10,512]{1,0:T(8,128)S(1)} %dynamic-slice_bitcast_fusion.15, pred[512,1024]{1,0:T(8,128)(4,1)S(1)} %broadcast_compare_fusion.4, bf16[1024,10,32]{0,2,1:T(8,128)(2,1)} %get-tuple-element.1032, ...), kind=kOutput, calls=%fused_computation.18.clone.1 | convolution fusion | flops 361753600 | bytes 43491332 | tf_op jit(solution)/shard_map/while/body/eval_jaxpr/while/body/eval_jaxpr/qhd,khd->hqk/dot_general | solution.py:69
  627.5 14.6 %multiply_convert_fusion.3 = bf16[10,512,1024]{2,1,0:T(8,128)(2,1)S(1)} fusion(f32[10,512,1024]{2,1,0:T(8,128)} %get-tuple-element.984, f32[10,512,1024]{2,1,0:T(8,128)} %copy-done, f32[10,512]{1,0:T(8,128)S(1)} %get-tuple-element.985, f32[10,512]{1,0:T(8,128)S(1)} %dynamic-slice_bitcast_fusion.15, pred[512,1024]{1,0:T(8,128)(4,1)S(1)} %broadcast_compare_fusion.4), kind=kLoop, calls=%fused_computation.17.clone.1 | loop fusion | flops 31457280 | bytes 52994048 | tf_op jit(solution)/shard_map/while/body/eval_jaxpr/while/body/eval_jaxpr/convert_element_type | solution.py:73
  668.1 15.2 %multiply_reduce_fusion.13 = (f32[10,512]{1,0:T(8,128)S(1)}, f32[10,512,1024]{2,1,0:T(8,128)}) fusion(f32[10,512,1024]{2,1,0:T(8,128)} %copy-done, f32[10,512]{1,0:T(8,128)S(1)} %dynamic-slice_bitcast_fusion.15, pred[512,1024]{1,0:T(8,128)(4,1)S(1)} %broadcast_compare_fusion.4, bf16[1024,10,32]{0,2,1:T(8,128)(2,1)} %get-tuple-element.1032, ...), kind=kOutput, calls=%fused_computation.18.clone.1 | convolution fusion | flops 361753600 | bytes 43491332 | tf_op jit(solution)/shard_map/while/body/eval_jaxpr/while/body/eval_jaxpr/qhd,khd->hqk/dot_general | solution.py:69
  683.3 14.6 %multiply_convert_fusion.3 = bf16[10,512,1024]{2,1,0:T(8,128)(2,1)S(1)} fusion(f32[10,512,1024]{2,1,0:T(8,128)} %get-tuple-element.984, f32[10,512,1024]{2,1,0:T(8,128)} %copy-done, f32[10,512]{1,0:T(8,128)S(1)} %get-tuple-element.985, f32[10,512]{1,0:T(8,128)S(1)} %dynamic-slice_bitcast_fusion.15, pred[512,1024]{1,0:T(8,128)(4,1)S(1)} %broadcast_compare_fusion.4), kind=kLoop, calls=%fused_computation.17.clone.1 | loop fusion | flops 31457280 | bytes 52994048 | tf_op jit(solution)/shard_map/while/body/eval_jaxpr/while/body/eval_jaxpr/convert_element_type | solution.py:73
  731.0 111.3 %while.58 = (s32[]{:T(128)}, f32[1024,10,32]{0,2,1:T(8,128)S(1)}, f32[1024,10,32]{0,2,1:T(8,128)}, f32[2,512,10,32]{1,3,2,0:T(8,128)}, bf16[2,512,10,32]{1,3,2,0...) while((s32[]{:T(128)}, f32[1024,10,32]{0,2,1:T(8,128)S(1)}, ...), condition=%wide.region_19.19_spmd.clone, body=%wide.region_17.18_spmd.clone.sunk | while | flops 1758686208 | bytes 255219920 | solution.py:110
  750.7 15.2 %multiply_reduce_fusion.13 = (f32[10,512]{1,0:T(8,128)S(1)}, f32[10,512,1024]{2,1,0:T(8,128)}) fusion(f32[10,512,1024]{2,1,0:T(8,128)} %copy-done, f32[10,512]{1,0:T(8,128)S(1)} %dynamic-slice_bitcast_fusion.15, pred[512,1024]{1,0:T(8,128)(4,1)S(1)} %broadcast_compare_fusion.4, bf16[1024,10,32]{0,2,1:T(8,128)(2,1)} %get-tuple-element.1032, ...), kind=kOutput, calls=%fused_computation.18.clone.1 | convolution fusion | flops 361753600 | bytes 43491332 | tf_op jit(solution)/shard_map/while/body/eval_jaxpr/while/body/eval_jaxpr/qhd,khd->hqk/dot_general | solution.py:69
  765.9 14.6 %multiply_convert_fusion.3 = bf16[10,512,1024]{2,1,0:T(8,128)(2,1)S(1)} fusion(f32[10,512,1024]{2,1,0:T(8,128)} %get-tuple-element.984, f32[10,512,1024]{2,1,0:T(8,128)} %copy-done, f32[10,512]{1,0:T(8,128)S(1)} %get-tuple-element.985, f32[10,512]{1,0:T(8,128)S(1)} %dynamic-slice_bitcast_fusion.15, pred[512,1024]{1,0:T(8,128)(4,1)S(1)} %broadcast_compare_fusion.4), kind=kLoop, calls=%fused_computation.17.clone.1 | loop fusion | flops 31457280 | bytes 52994048 | tf_op jit(solution)/shard_map/while/body/eval_jaxpr/while/body/eval_jaxpr/convert_element_type | solution.py:73
  806.5 15.2 %multiply_reduce_fusion.13 = (f32[10,512]{1,0:T(8,128)S(1)}, f32[10,512,1024]{2,1,0:T(8,128)}) fusion(f32[10,512,1024]{2,1,0:T(8,128)} %copy-done, f32[10,512]{1,0:T(8,128)S(1)} %dynamic-slice_bitcast_fusion.15, pred[512,1024]{1,0:T(8,128)(4,1)S(1)} %broadcast_compare_fusion.4, bf16[1024,10,32]{0,2,1:T(8,128)(2,1)} %get-tuple-element.1032, ...), kind=kOutput, calls=%fused_computation.18.clone.1 | convolution fusion | flops 361753600 | bytes 43491332 | tf_op jit(solution)/shard_map/while/body/eval_jaxpr/while/body/eval_jaxpr/qhd,khd->hqk/dot_general | solution.py:69
  821.6 14.6 %multiply_convert_fusion.3 = bf16[10,512,1024]{2,1,0:T(8,128)(2,1)S(1)} fusion(f32[10,512,1024]{2,1,0:T(8,128)} %get-tuple-element.984, f32[10,512,1024]{2,1,0:T(8,128)} %copy-done, f32[10,512]{1,0:T(8,128)S(1)} %get-tuple-element.985, f32[10,512]{1,0:T(8,128)S(1)} %dynamic-slice_bitcast_fusion.15, pred[512,1024]{1,0:T(8,128)(4,1)S(1)} %broadcast_compare_fusion.4), kind=kLoop, calls=%fused_computation.17.clone.1 | loop fusion | flops 31457280 | bytes 52994048 | tf_op jit(solution)/shard_map/while/body/eval_jaxpr/while/body/eval_jaxpr/convert_element_type | solution.py:73
  912.9 48.7 %all-reduce.14.cloned.1.call-done = bf16[2048,640]{1,0:T(8,128)(2,1)} async-done(((bf16[2048,640]{1,0:T(8,128)(2,1)}), bf16[2048,640]{1,0:T(8,128)(2,1)}) %all-reduce.14.cloned.1.call-update) | async-done | bytes 2621456 | tf_op jit(solution)/shard_map/psum | solution.py:245
  968.4 56.1 %all-reduce.3 = (f32[3,320]{1,0:T(4,128)S(1)}, f32[1280]{0:T(1024)S(1)}, f32[6,640]{1,0:T(8,128)S(1)}) all-reduce(f32[3,320]{1,0:T(4,128)S(1)} %convert_reduce_fusion.2, f32[1280]{0:T(1024)S(1)} %copy-done.68, f32[6,640]{1,0:T(8,128)S(1)} %stack.48), channel_id=1, replica_groups=mesh['dp'=16,'tp'=2] {'dp'}, use_global_device_ids=true, to_apply=%region_35.36 | all-reduce | flops 6080 | bytes 48640 | tf_op jit(solution)/shard_map/psum | solution.py:265
  1035.9 133.0 %all-reduce.16.cloned.1.call-done = (f32[4,640,320]{2,1,0:T(8,128)}, f32[2,640,1280]{2,1,0:T(8,128)}) async-done(((f32[4,640,320]{2,1,0:T(8,128)}, f32[2,640,1280]{2,1,0:T(8,128)}), (f32[4,640,320]{2,1,0:T(8,128)}, f32[2,640,1280]{2,1,0:T(8,128)})) %all-reduce.16.cloned.1.call-update) | async-done | bytes 9830416 | tf_op jit(solution)/shard_map/psum | solution.py:265
  1174.3 40.2 %all-reduce.2 = (f32[16]{0:T(128)S(1)}, f32[16]{0:T(128)S(1)}) all-reduce(f32[16]{0:T(128)S(1)} %concatenate.39, f32[16]{0:T(128)S(1)} %concatenate.37), channel_id=1, replica_groups=mesh['dp'=16,'tp'=2] {'dp','tp'}, use_global_device_ids=true, to_apply=%region_48.49 | all-reduce | flops 32 | bytes 256 | tf_op jit(solution)/shard_map/psum | solution.py:281
  (413 shorter events, 436.4 us)
Async XLA Ops:
  7.2 44.7 %all-gather.5.cloned.1.call-start = ((), (), s32[]{:S(2)}) async-start(), calls=%async_computation | async-start | bytes 2088960 | tf_op jit(solution)/shard_map/all_gather | solution.py:164
  9.1 307.0 %all-reduce.10.cloned.1.call-start = ((), (), s32[]{:S(2)}) async-start(), calls=%async_computation.1 | async-start | bytes 5242880 | tf_op jit(solution)/shard_map/psum | solution.py:187
  13.8 69.5 %copy-start.27 = (f32[2,1024,32]{1,2,0:T(8,128)}, f32[2,1024,32]{1,2,0:T(8,128)S(1)}, u32[]{:S(2)}) copy-start(f32[2,1024,32]{1,2,0:T(8,128)S(1)} %get-tuple-element.689) | copy-start | bytes 786436
  13.8 69.5 %copy-start.29 = (f32[2,1024,32]{1,2,0:T(8,128)}, f32[2,1024,32]{1,2,0:T(8,128)S(1)}, u32[]{:S(2)}) copy-start(f32[2,1024,32]{1,2,0:T(8,128)S(1)} %get-tuple-element.690) | copy-start | bytes 786436
  92.6 54.8 %copy-start.37 = (f32[2,2,10,512]{3,2,1,0:T(8,128)S(1)}, f32[2,2,10,512]{3,2,1,0:T(8,128)}, u32[]{:S(2)}) copy-start(f32[2,2,10,512]{3,2,1,0:T(8,128)} %get-tuple-element.1074) | copy-start | bytes 245764 | tf_op jit(solution)/shard_map/while
  161.9 54.8 %copy-start.37 = (f32[2,2,10,512]{3,2,1,0:T(8,128)S(1)}, f32[2,2,10,512]{3,2,1,0:T(8,128)}, u32[]{:S(2)}) copy-start(f32[2,2,10,512]{3,2,1,0:T(8,128)} %get-tuple-element.1074) | copy-start | bytes 245764 | tf_op jit(solution)/shard_map/while
  237.8 78.3 %copy-start.4 = (bf16[2048,640]{1,0:T(8,128)(2,1)S(1)}, bf16[2048,640]{1,0:T(8,128)(2,1)}, u32[]{:S(2)}) copy-start(bf16[2048,640]{1,0:T(8,128)(2,1)} %param.26) | copy-start | bytes 7864324
  237.8 78.3 %copy-start.43 = (f32[640]{0:T(1024)S(1)}, f32[640]{0:T(1024)}, u32[]{:S(2)}) copy-start(f32[640]{0:T(1024)} %get-tuple-element.569) | copy-start | bytes 7684
  242.6 123.9 %all-gather.7.cloned.1.call-start = ((), (), s32[]{:S(2)}) async-start(), calls=%async_computation.2 | async-start | bytes 3481600 | tf_op jit(solution)/shard_map/all_gather | solution.py:165
  243.4 246.9 %all-reduce.12.cloned.1.call-start = ((), (), s32[]{:S(2)}) async-start(), calls=%async_computation.3 | async-start | bytes 5242880 | tf_op jit(solution)/shard_map/psum | solution.py:216
  418.2 142.6 %all-gather.9.cloned.1.call-start = ((), (), s32[]{:S(2)}) async-start(), calls=%async_computation.5 | async-start | bytes 7864320 | tf_op jit(solution)/shard_map/all_gather | solution.py:201
  427.1 534.5 %all-reduce.14.cloned.1.call-start = ((), (), s32[]{:S(2)}) async-start(), calls=%async_computation.4 | async-start | bytes 5242880 | tf_op jit(solution)/shard_map/psum | solution.py:245
  500.1 66.4 %copy-start.61 = (f32[640]{0:T(1024)S(1)}, f32[640]{0:T(1024)}, u32[]{:S(2)}) copy-start(f32[640]{0:T(1024)} %get-tuple-element.566) | copy-start | bytes 7684
  887.1 281.8 %all-reduce.16.cloned.1.call-start = ((), (), s32[]{:S(2)}) async-start(), calls=%async_computation.6 | async-start | bytes 20971520 | tf_op jit(solution)/shard_map/psum | solution.py:265
  909.3 56.0 %copy-start.48 = (f32[2048]{0:T(1024)S(1)}, f32[2048]{0:T(1024)}, u32[]{:S(2)}) copy-start(f32[2048]{0:T(1024)} %copy-done.47) | copy-start | bytes 24580
  912.8 55.7 %copy-start.68 = (f32[1280]{0:T(1024)S(1)}, f32[1280]{0:T(1024)}, u32[]{:S(2)}) copy-start(f32[1280]{0:T(1024)} %get-tuple-element.696) | copy-start | bytes 15364
  912.8 111.8 %copy-start.53 = (f32[1280]{0:T(1024)S(1)}, f32[1280]{0:T(1024)}, u32[]{:S(2)}) copy-start(f32[1280]{0:T(1024)} %param.32) | copy-start | bytes 15364
  912.8 111.8 %copy-start.66 = (f32[1280]{0:T(1024)S(1)}, f32[1280]{0:T(1024)}, u32[]{:S(2)}) copy-start(f32[1280]{0:T(1024)} %param.37) | copy-start | bytes 15364
  912.8 111.8 %copy-start.67 = (f32[1280]{0:T(1024)S(1)}, f32[1280]{0:T(1024)}, u32[]{:S(2)}) copy-start(f32[1280]{0:T(1024)} %param.42) | copy-start | bytes 15364
  912.8 114.3 %copy-start.42 = (f32[6,640]{1,0:T(8,128)S(1)}, f32[6,640]{1,0:T(8,128)}, u32[]{:S(2)}) copy-start(f32[6,640]{1,0:T(8,128)} %param.33) | copy-start | bytes 46084
  912.8 114.3 %copy-start.59 = (f32[6,640]{1,0:T(8,128)S(1)}, f32[6,640]{1,0:T(8,128)}, u32[]{:S(2)}) copy-start(f32[6,640]{1,0:T(8,128)} %param.38) | copy-start | bytes 46084
  912.8 114.2 %copy-start.60 = (f32[6,640]{1,0:T(8,128)S(1)}, f32[6,640]{1,0:T(8,128)}, u32[]{:S(2)}) copy-start(f32[6,640]{1,0:T(8,128)} %param.43) | copy-start | bytes 46084
  912.8 115.6 %copy-start.58 = (f32[3,320]{1,0:T(4,128)S(1)}, f32[3,320]{1,0:T(4,128)}, u32[]{:S(2)}) copy-start(f32[3,320]{1,0:T(4,128)} %param.31) | copy-start | bytes 11524
  912.9 115.6 %copy-start.69 = (f32[3,320]{1,0:T(4,128)S(1)}, f32[3,320]{1,0:T(4,128)}, u32[]{:S(2)}) copy-start(f32[3,320]{1,0:T(4,128)} %param.36) | copy-start | bytes 11524
  912.9 115.6 %copy-start.70 = (f32[3,320]{1,0:T(4,128)S(1)}, f32[3,320]{1,0:T(4,128)}, u32[]{:S(2)}) copy-start(f32[3,320]{1,0:T(4,128)} %param.41) | copy-start | bytes 11524
  1030.3 138.7 %copy-start.31 = (f32[4,40,320]{2,1,0:T(8,128)S(1)}, f32[4,40,320]{2,1,0:T(8,128)}, u32[]{:S(2)}) copy-start(f32[4,40,320]{2,1,0:T(8,128)} %param.29) | copy-start | bytes 614404
  1030.3 138.7 %copy-start.39 = (f32[4,40,320]{2,1,0:T(8,128)S(1)}, f32[4,40,320]{2,1,0:T(8,128)}, u32[]{:S(2)}) copy-start(f32[4,40,320]{2,1,0:T(8,128)} %param.34) | copy-start | bytes 614404
  1030.3 140.0 %copy-start.24 = (f32[2,40,1280]{2,1,0:T(8,128)S(1)}, f32[2,40,1280]{2,1,0:T(8,128)}, u32[]{:S(2)}) copy-start(f32[2,40,1280]{2,1,0:T(8,128)} %param.30) | copy-start | bytes 1228804
  1035.9 185.5 %copy-start.54 = (f32[1280]{0:T(1024)S(1)}, f32[1280]{0:T(1024)}, u32[]{:S(2)}) copy-start(f32[1280]{0:T(1024)} %param.32) | copy-start | bytes 15364
  1035.9 185.5 %copy-start.55 = (f32[1280]{0:T(1024)S(1)}, f32[1280]{0:T(1024)}, u32[]{:S(2)}) copy-start(f32[1280]{0:T(1024)} %get-tuple-element.659) | copy-start | bytes 15364
  1035.9 185.5 %copy-start.56 = (f32[1280]{0:T(1024)S(1)}, f32[1280]{0:T(1024)}, u32[]{:S(2)}) copy-start(f32[1280]{0:T(1024)} %get-tuple-element.660) | copy-start | bytes 15364
  1170.3 52.7 %copy-start.36 = (f32[4,40,320]{2,1,0:T(8,128)}, f32[4,40,320]{2,1,0:T(8,128)S(1)}, u32[]{:S(2)}) copy-start(f32[4,40,320]{2,1,0:T(8,128)S(1)} %get-tuple-element.669) | copy-start | bytes 614404
  (70 other events, 867.7 us)
Sparse Core Ops, SparseCore 0:
  10.9 40.9 all-gather.4
  242.7 73.3 all-reduce.9
  319.1 47.3 all-gather.6
  418.4 71.8 all-reduce.11
  492.2 68.5 all-gather.8
  887.2 74.3 all-reduce.13
  965.9 202.9 all-reduce.15
